TPU v7x, 32 devices: a whole 2x2x4 slice. The times are simulated.
32 devices in a mesh: row: 2 (over x), col: 16 (over z, y, core).
Axes of the slice: x: 2, y: 2, z: 4, core: 2. Of those that a mesh axis runs over, the one named last changes fastest.
Arguments:
- features: bfloat16 [8192, 256], P(('row', 'col')), may hold values from -6 to 6
- weight: bfloat16 [256, 128], replicated, may hold values from -0.375 to 0.375
- tiles: bfloat16 [2, 16, 320, 128, 128], P('row', 'col'), may hold values from -0.0625 to 0.0625
- slot_tile_row: int32 [2, 16, 320], P('row', 'col'), may hold values from 0 to 3
- tile_cols: int32 [2, 16, 320], P('row', 'col'), may hold values from 0 to 31
- live_tiles: int32 [2, 16], P('row', 'col'), may hold values from 40 to 320, as said below
- cotangent: bfloat16 [8192, 128], P(('row', 'col')), may hold values from -6 to 6
Outputs:
- logits: bfloat16 [8192, 128], P(('row', 'col'))
- grad_features: bfloat16 [8192, 256], P(('row', 'col'))
- grad_weight: float32 [256, 128], replicated
Inputs may be any that keep to these rules, and one draw needn't show every extreme that they name: Slots of a block from live_tiles on are padding and not part of the adjacency; in every draw some block has all 320 slots live.
All inputs are finite; a program needn't handle non-finite values.
Results may differ from a plain program's by a relative error of at most 0.005.
Values may be sent and summed in bfloat16 or wider, within the bound.
A program may use at most 128 MiB of HBM per device.

v0:
```python
import functools
import math

import jax
import jax.numpy as jnp
from jax import lax
from jax.experimental import pallas as pl
from jax.experimental.pallas import tpu as pltpu
from jax.sharding import PartitionSpec as P

MESH = pl.DeviceIdType.MESH
F32 = jnp.float32
BF16 = jnp.bfloat16


def kernel(dims, features, weight, tiles, slot_rows, slot_cols, live, cot,
           logits, grad_features, grad_weight,
           tile_buf, sums, proj, cots, cots_t, feat_t, code_v, last_v, code, last,
           sib_out, sib_in, y_out, y_in, z_out, z_in, log_out, log_in,
           term_out, term_in, total,
           tile_sem, smem_sem, cot_send, cot_recv, ag_send, ag_recv,
           sib_send, sib_recv, y_send, y_recv, z_send, z_recv,
           log_send, log_recv, term_send, term_recv, tot_send, tot_recv):
    R, C, O, I = dims
    n = R * C
    slots = tiles.shape[0]
    side = tiles.shape[1]
    stretch = features.shape[0]
    per = stretch // side
    col_tiles = C * per
    cells = R * per * col_tiles
    r, c = lax.axis_index("row"), lax.axis_index("col")
    me = r * C + c
    k = lax.rem(c, 2)
    q = c // 2
    y = lax.rem(q, I)
    z = q // I

    def col_of(zz, yy, kk):
        return (zz * I + yy) * 2 + kk

    def remote(src, dst, send, recv, dev):
        return pltpu.make_async_remote_copy(
            src_ref=src, dst_ref=dst, send_sem=send, recv_sem=recv,
            device_id=dev, device_id_type=MESH)

    chunks = tile_sem.shape[0]
    chunk = slots // chunks
    loads = [
        pltpu.make_async_copy(tiles.at[pl.ds(i * chunk, chunk)],
                              tile_buf.at[pl.ds(i * chunk, chunk)], tile_sem.at[i])
        for i in range(chunks)
    ]
    for load in loads:
        load.start()

    barrier = pltpu.get_barrier_semaphore()

    def greet(d, carry):
        t = lax.rem(me + d, n)
        pl.semaphore_signal(barrier, inc=1, device_id=(t // C, lax.rem(t, C)), device_id_type=MESH)
        return carry

    lax.fori_loop(1, n, greet, 0, unroll=n - 1 if n <= 32 else 1)
    proj[c] = jnp.dot(features[...], weight[...], preferred_element_type=F32).astype(BF16)
    lane = lax.broadcasted_iota(jnp.int32, (1, slots), 1)
    cell = jnp.where(lane < live[0, 0], slot_rows[...] * col_tiles + slot_cols[...], cells)
    eye = (lax.broadcasted_iota(jnp.int32, (slots, slots), 0)
           == lax.broadcasted_iota(jnp.int32, (slots, slots), 1))
    cell_c = jnp.sum(jnp.where(eye, cell, 0), axis=1, keepdims=True)
    sub = lax.broadcasted_iota(jnp.int32, (slots, 1), 0)
    same_before = (cell == cell_c) & (lane < sub)
    rank = jnp.sum(((cell < cell_c) | same_before).astype(jnp.int32), axis=1, keepdims=True)
    keep = jnp.max(same_before.astype(jnp.int32), axis=1, keepdims=True)
    code_v[...] = jnp.sum(jnp.where(rank == lane, sub * 2 + keep, 0), axis=0, keepdims=True)
    cell_ids = lax.broadcasted_iota(jnp.int32, (1, cells), 1)
    upto = jnp.sum((cell_c <= cell_ids).astype(jnp.int32), axis=0, keepdims=True)
    held = jnp.max((cell_c == cell_ids).astype(jnp.int32), axis=0, keepdims=True)
    last_v[...] = upto * held
    to_smem = [pltpu.make_async_copy(code_v, code, smem_sem.at[0]),
               pltpu.make_async_copy(last_v, last, smem_sem.at[1])]
    for copy in to_smem:
        copy.start()
    feat_t[...] = features[...].astype(F32).T.astype(BF16)
    cots_t[r] = cot[...].astype(F32).T.astype(BF16)
    sums[0] = jnp.zeros((side, side), BF16)
    pl.semaphore_wait(barrier, n - 1)

    pending = []

    def gather_send(block, dev):
        copy = remote(proj.at[block], proj.at[block], ag_send.at[len(pending)],
                      ag_recv.at[block], (r, dev))
        copy.start()
        pending.append(copy)

    def gather_wait(block):
        remote(proj.at[block], proj.at[block], ag_send.at[0], ag_recv.at[block],
               (r, c)).wait_recv()

    cot_copies = []
    for d in range(1, R):
        peer = lax.rem(r + d, R)
        copy = remote(cot, cots.at[r], cot_send.at[d], cot_recv.at[r], (peer, c))
        copy.start()
        cot_copies.append(copy)
    z_peers = [lax.rem(z + d, O) for d in range(1, O)]
    y_peers = [lax.rem(y + d, I) for d in range(1, I)]
    for yy in y_peers:
        gather_send(c, col_of(z, yy, k))
    for zz in z_peers:
        gather_send(c, col_of(zz, y, k))
    gather_send(c, col_of(z, y, 1 - k))

    for copy in to_smem:
        copy.wait()
    for load in loads:
        load.wait()

    def add_slot(j, acc):
        word = code[0, j]
        keep_it = lax.rem(word, 2).astype(F32)
        acc = acc * keep_it + tile_buf[word // 2].astype(F32)
        sums[j + 1] = acc.astype(BF16)
        return acc

    parts = 8
    acc = jnp.zeros((side, side), F32)
    for part in range(parts):
        acc = lax.fori_loop(part * slots // parts, (part + 1) * slots // parts, add_slot, acc,
                            unroll=4)
        for zz in z_peers[part - 2:part - 1] if part > 1 else []:
            block = col_of(zz, y, k)
            gather_wait(block)
            for yy in y_peers:
                gather_send(block, col_of(z, yy, k))
            gather_send(block, col_of(z, y, 1 - k))

    for d in range(1, R):
        peer = lax.rem(r + d, R)
        remote(cot, cots.at[peer], cot_send.at[d], cot_recv.at[peer], (peer, c)).wait_recv()
        cots_t[peer] = cots[peer].astype(F32).T.astype(BF16)

    def stretch_block(s, b):
        rows = []
        for a in range(per):
            base = (s * per + a) * col_tiles + b * per
            rows.append(jnp.concatenate([sums[last[0, base + e]] for e in range(per)], axis=1))
        return jnp.concatenate(rows, axis=0)

    def back_block(b):
        out = jnp.dot(cots_t[0], stretch_block(0, b), preferred_element_type=F32)
        for s in range(1, R):
            out = out + jnp.dot(cots_t[s], stretch_block(s, b), preferred_element_type=F32)
        return out

    def place(i):
        zz = lax.rem(z + lax.rem(i, O) + 1, O)
        yy = lax.rem(y + i // O + 1, I)
        return zz, yy

    def sib_copy(m):
        return remote(sib_out.at[m], sib_in.at[m], sib_send.at[m], sib_recv.at[m],
                      (r, col_of(z, y, 1 - k)))

    def send_sib(i, carry):
        zz, yy = place(i)
        m = zz * I + yy
        sib_out[m] = back_block(2 * m + 1 - k).astype(BF16)
        sib_copy(m).start()
        return carry

    lax.fori_loop(0, O * I, send_sib, 0)

    def y_copy(zz, yy):
        return remote(y_out.at[zz * I + yy], y_in.at[y * O + zz], y_send.at[zz * I + yy],
                      y_recv.at[y * O + zz], (r, col_of(z, yy, k)))

    def send_y(i, carry):
        zz, yy = place(i)
        m = zz * I + yy
        mine = back_block(2 * m + k)
        sib_copy(m).wait_recv()
        y_out[m] = (mine + sib_in[m].astype(F32)).astype(BF16)
        y_copy(zz, yy).start()
        return carry

    lax.fori_loop(0, O * (I - 1), send_y, 0)

    for d in range(O):
        zz = lax.rem(z + d, O)
        for yy in y_peers:
            block = col_of(zz, yy, k)
            gather_wait(block)
            gather_send(block, col_of(z, y, 1 - k))

    def summed(zz):
        m = zz * I + y
        value = back_block(2 * m + k)
        sib_copy(m).wait_recv()
        value = value + sib_in[m].astype(F32)
        for yy in y_peers:
            slot = yy * O + zz
            remote(y_out.at[0], y_in.at[slot], y_send.at[0], y_recv.at[slot],
                   (r, c)).wait_recv()
            value = value + y_in[slot].astype(F32)
        return value

    z_copies = []
    for d in range(1, O):
        zz = lax.rem(z + d, O)
        z_out[d - 1] = summed(zz).astype(BF16)
        copy = remote(z_out.at[d - 1], z_in.at[z], z_send.at[d - 1], z_recv.at[z],
                      (r, col_of(zz, y, k)))
        copy.start()
        z_copies.append(copy)
    for d in range(O):
        for e in range(I):
            gather_wait(col_of(lax.rem(z + d, O), lax.rem(y + e, I), 1 - k))
    group = 4 if C % 4 == 0 else 1

    def forward(s):
        def step(g, out):
            for b in range(group):
                out = out + jnp.dot(stretch_block(s, g * group + b), proj[g * group + b],
                                    preferred_element_type=F32)
            return out
        return lax.fori_loop(0, C // group, step, jnp.zeros((stretch, proj.shape[2]), F32))

    log_copies = []
    for d in range(1, R):
        peer = lax.rem(r + d, R)
        log_out[d - 1] = forward(peer)
        copy = remote(log_out.at[d - 1], log_in.at[r], log_send.at[d], log_recv.at[r], (peer, c))
        copy.start()
        log_copies.append(copy)
    mine_log = forward(r)

    back_t = summed(z)
    for zz in z_peers:
        remote(z_out.at[0], z_in.at[zz], z_send.at[0], z_recv.at[zz], (r, c)).wait_recv()
        back_t = back_t + z_in[zz].astype(F32)
    back = back_t.T.astype(BF16)
    term = jnp.dot(feat_t[...], back, preferred_element_type=F32)

    owners = term_out.shape[0]
    rows = term_out.shape[1]
    term_out[...] = term.reshape(term_out.shape).astype(BF16)

    def term_copy(t):
        return remote(term_out.at[t], term_in.at[me], term_send.at[0], term_recv.at[0],
                      (t // C, lax.rem(t, C)))

    def bulk(count, send, recv):
        part = (term_in if send is term_send else total).at[pl.ds(0, count)]
        return remote(part, part, send.at[0], recv.at[0], (r, c))

    def arrived(count, send, recv):
        bulk(count, send, recv).wait_recv()

    def sent(count, send, recv):
        bulk(count, send, recv).wait_send()

    def by_role(act, send, recv):
        if owners == n:
            act(n - 1, send, recv)
        else:
            pl.when(me < owners)(lambda: act(owners - 1, send, recv))
            pl.when(me >= owners)(lambda: act(owners, send, recv))

    def tot_copy(t):
        return remote(total.at[me], total.at[me], tot_send.at[0], tot_recv.at[0],
                      (t // C, lax.rem(t, C)))

    def others(count, act):
        def body(d, carry):
            t = lax.rem(me + d, n)
            if count == n:
                act(t)
            else:
                @pl.when(t < count)
                def _():
                    act(t)
            return carry
        lax.fori_loop(1, n, body, 0, unroll=n - 1 if n <= 32 else 1)

    def own_part():
        term_in[me] = term_out[me]
        arrived(n - 1, term_send, term_recv)
        total[me] = jnp.sum(term_in[...].astype(F32), axis=0) * (1.0 / math.sqrt(n * stretch))
        others(n, lambda t: tot_copy(t).start())

    others(owners, lambda t: term_copy(t).start())
    grad_features[...] = lax.dot_general(
        back, weight[...], (((1,), (1,)), ((), ())), preferred_element_type=F32).astype(BF16)
    for d in range(1, R):
        peer = lax.rem(r + d, R)
        remote(log_out.at[0], log_in.at[peer], log_send.at[0], log_recv.at[peer],
               (peer, c)).wait_recv()
        mine_log = mine_log + log_in[peer]
    logits[...] = mine_log.astype(BF16)
    if owners == n:
        own_part()
    else:
        pl.when(me < owners)(own_part)
    for copy in pending + cot_copies + log_copies + z_copies:
        copy.wait_send()

    def drain_sib(m, carry):
        sib_copy(m).wait_send()
        return carry

    lax.fori_loop(0, O * I, drain_sib, 0)

    def drain_y(i, carry):
        zz, yy = place(i)
        y_copy(zz, yy).wait_send()
        return carry

    lax.fori_loop(0, O * (I - 1), drain_y, 0)
    by_role(sent, term_send, term_recv)
    by_role(arrived, tot_send, tot_recv)
    grad_weight[...] = total[pl.ds(0, owners)].reshape(grad_weight.shape)
    if owners == n:
        sent(n - 1, tot_send, tot_recv)
    else:
        @pl.when(me < owners)
        def _():
            sent(n - 1, tot_send, tot_recv)


def hand_over(a, b, c, x, y, z):
    x[...] = a[...]
    y[...] = b[...]
    z[...] = c[...]


def per_device(R, C, features, weight, tiles, slot_tile_row, tile_cols, live_tiles, cotangent):
    slots, side = tiles.shape[2], tiles.shape[3]
    stretch, width = features.shape
    out_width = weight.shape[1]
    half = C // 2
    O = 4 if half % 4 == 0 else half
    I = half // O
    n = R * C
    per = stretch // side
    cells = R * per * C * per
    owners = min(n, width // 8)
    rows = width // owners
    chunks = 8 if slots % 8 == 0 else 1
    dma = pltpu.SemaphoreType.DMA
    vmem = pltpu.VMEM
    blk = (out_width, stretch)
    gathers = (O - 1) + (I - 1) + 1 + (O - 1) * I + O * (I - 1)
    scratch = [
        vmem((slots, side, side), BF16),
        vmem((slots + 1, side, side), BF16),
        vmem((C, stretch, out_width), BF16),
        vmem((R, stretch, out_width), BF16),
        vmem((R,) + blk, BF16),
        vmem((width, stretch), BF16),
        vmem((1, slots), jnp.int32),
        vmem((1, cells), jnp.int32),
        pltpu.SMEM((1, slots), jnp.int32),
        pltpu.SMEM((1, cells), jnp.int32),
        vmem((half,) + blk, BF16),
        vmem((half,) + blk, BF16),
        vmem((half,) + blk, BF16),
        vmem((half,) + blk, BF16),
        vmem((max(O - 1, 1),) + blk, BF16),
        vmem((O,) + blk, BF16),
        vmem((max(R - 1, 1), stretch, out_width), F32),
        vmem((R, stretch, out_width), F32),
        vmem((owners, rows, out_width), BF16),
        vmem((n, rows, out_width), BF16),
        vmem((n, rows, out_width), F32),
        dma((chunks,)), dma((2,)), dma((R,)), dma((R,)),
        dma((gathers,)), dma((C,)),
        dma((half,)), dma((half,)), dma((half,)), dma((half,)),
        dma((O,)), dma((O,)), dma((R,)), dma((R,)),
        dma((1,)), dma((1,)), dma((1,)), dma((1,)),
    ]
    v = pl.BlockSpec(memory_space=pltpu.VMEM)
    shapes = (
            jax.ShapeDtypeStruct((stretch, out_width), BF16),
            jax.ShapeDtypeStruct((stretch, width), BF16),
            jax.ShapeDtypeStruct((width, out_width), F32),
        )
    results = pl.pallas_call(
        functools.partial(kernel, (R, C, O, I)),
        out_shape=shapes,
        in_specs=[v, v, pl.BlockSpec(memory_space=pl.ANY), v, v,
                  pl.BlockSpec(memory_space=pltpu.SMEM), v],
        out_specs=(v, v, v),
        scratch_shapes=scratch,
        compiler_params=pltpu.CompilerParams(
            collective_id=0, has_side_effects=True, vmem_limit_bytes=60 * 1024 * 1024),
    )(features, weight, tiles.reshape(slots, side, side), slot_tile_row.reshape(1, slots),
      tile_cols.reshape(1, slots), live_tiles, cotangent)
    return pl.pallas_call(hand_over, out_shape=shapes, in_specs=[v, v, v],
                          out_specs=(v, v, v))(*results)


def solution(mesh):
    R, C = mesh.shape["row"], mesh.shape["col"]
    placed = (
        P(("row", "col"), None),
        P(),
        P("row", "col", None, None, None),
        P("row", "col", None),
        P("row", "col", None),
        P("row", "col"),
        P(("row", "col"), None),
    )
    return jax.shard_map(
        functools.partial(per_device, R, C),
        mesh=mesh,
        in_specs=placed,
        out_specs=(P(("row", "col"), None), P(("row", "col"), None), P()),
        check_vma=False,
    )
```

profile of v0, /device:TPU:0, one launch (start us, length us, event | category | flops | bytes accessed | tf_op | source)
XLA Modules:
  0.0 43.1 jit_solution(12762327344969330123)
XLA Ops:
  1.3 40.0 %shard_map.94 = (bf16[256,128]{1,0:T(8,128)(2,1)}, bf16[256,256]{1,0:T(8,128)(2,1)}, f32[256,128]{1,0:T(8,128)}) custom-call(bf16[256,256]{1,0:T(8,128)(2,1)} %features.1, bf16[256,128]{1,0:T(8,128)(2,1)} %weight.1, bf16[320,128,128]{2,1,0:T(8,128)(2,1)} %bitcast.3, s32[1,320]{1,0:T(1,128)} %bitcast.4, s32[1,320]{1,0:T(1,128)} %bitcast.5, ...), custom_call_target="tpu_custom_call" | custom-call | tf_op jit(solution)/shard_map/pallas_call | solution.py:389
  41.3 1.7 %shard_map.95 = (bf16[256,128]{1,0:T(8,128)(2,1)}, bf16[256,256]{1,0:T(8,128)(2,1)}, f32[256,128]{1,0:T(8,128)}) custom-call(bf16[256,128]{1,0:T(8,128)(2,1)} %get-tuple-element.6.a, bf16[256,256]{1,0:T(8,128)(2,1)} %get-tuple-element.7.b, f32[256,128]{1,0:T(8,128)} %get-tuple-element.8.c), custom_call_target="tpu_custom_call" | custom-call | tf_op jit(solution)/shard_map/pallas_call | solution.py:400
where the time goes:
time: 43.2 us; the launch traced here: 43.1 us
  Pallas kernels  41.8 us (97%)
  between operations  1.29 us (3%)
    pallas_call x1, Pallas kernels, per_device(): pl.pallas_call(functools.partial(kernel, (R, C, O, I)), out_shape=shapes,...  40 us
    pallas_call x1, Pallas kernels, per_device(): pl.pallas_call(hand_over, out_shape=shapes, in_specs=[v, v, v], out_specs...  1.73 us

commit v1 on v0

v1 whole, which is shorter than its diff:
```python
import functools
import math

import jax
import jax.numpy as jnp
from jax import lax
from jax.experimental import pallas as pl
from jax.experimental.pallas import tpu as pltpu
from jax.sharding import PartitionSpec as P

MESH = pl.DeviceIdType.MESH
F32 = jnp.float32
BF16 = jnp.bfloat16


def kernel(dims, features_h, weight_h, tiles, rows_h, cols_h, live, cot_h,
           logits, grad_features, grad_weight,
           features, weight, slot_rows, slot_cols,
           tile_buf, sums, dense, proj, cots, cots_t, feat_t, code_v, last_v, code, last,
           sib_out, sib_in, y_out, y_in, z_out, z_in, log_out, log_in,
           term_out, term_in, total,
           tile_sem, in_sem, smem_sem, cot_send, cot_recv, ag_send, ag_recv,
           sib_send, sib_recv, y_send, y_recv, z_send, z_recv,
           log_send, log_recv, term_send, term_recv, tot_send, tot_recv):
    R, C, O, I = dims
    n = R * C
    slots = tiles.shape[0]
    side = tiles.shape[1]
    stretch = features.shape[0]
    per = stretch // side
    row_tiles = R * per
    block_cells = row_tiles * per
    cells = C * block_cells
    r, c = lax.axis_index("row"), lax.axis_index("col")
    me = r * C + c
    k = lax.rem(c, 2)
    q = c // 2
    y = lax.rem(q, I)
    z = q // I

    def col_of(zz, yy, kk):
        return (zz * I + yy) * 2 + kk

    def remote(src, dst, send, recv, dev):
        return pltpu.make_async_remote_copy(
            src_ref=src, dst_ref=dst, send_sem=send, recv_sem=recv,
            device_id=dev, device_id_type=MESH)

    inputs = [
        pltpu.make_async_copy(src, dst, in_sem.at[i])
        for i, (src, dst) in enumerate((
            (rows_h, slot_rows), (cols_h, slot_cols),
            (features_h, features), (weight_h, weight), (cot_h, cots.at[r])))
    ]
    for copy in inputs:
        copy.start()
    chunks = tile_sem.shape[0]
    chunk = slots // chunks
    loads = [
        pltpu.make_async_copy(tiles.at[pl.ds(i * chunk, chunk)],
                              tile_buf.at[pl.ds(i * chunk, chunk)], tile_sem.at[i])
        for i in range(chunks)
    ]
    for load in loads[:0]:
        load.start()

    x_peers = [lax.rem(r + d, R) for d in range(1, R)]
    y_peers = [lax.rem(y + d, I) for d in range(1, I)]
    z_peers = [lax.rem(z + d, O) for d in range(1, O)]
    near = ([(peer, c) for peer in x_peers] + [(r, col_of(z, yy, k)) for yy in y_peers]
            + [(r, col_of(zz, y, k)) for zz in z_peers] + [(r, col_of(z, y, 1 - k))])
    barrier = pltpu.get_barrier_semaphore()
    with jax.named_scope("S00greet"):
        for dev in near:
            pl.semaphore_signal(barrier, inc=1, device_id=dev, device_id_type=MESH)

    with jax.named_scope("S01idx"):
        for copy in inputs[:2]:
            copy.wait()
    with jax.named_scope("S01rest"):
        for load in loads[0:]:
            load.start()
    with jax.named_scope("S02sort"):
        lane = lax.broadcasted_iota(jnp.int32, (1, slots), 1)
        col = slot_cols[...]
        where = (col // per) * block_cells + slot_rows[...] * per + lax.rem(col, per)
        cell = jnp.where(lane < live[0, 0], where, cells)
        eye = (lax.broadcasted_iota(jnp.int32, (slots, slots), 0)
               == lax.broadcasted_iota(jnp.int32, (slots, slots), 1))
        cell_c = jnp.sum(jnp.where(eye, cell, 0), axis=1, keepdims=True)
        sub = lax.broadcasted_iota(jnp.int32, (slots, 1), 0)
        before = (cell < cell_c) | ((cell == cell_c) & (lane < sub))
        rank = jnp.sum(before.astype(jnp.int32), axis=1, keepdims=True)
        code_v[...] = jnp.sum(jnp.where(rank == lane, sub, 0), axis=0, keepdims=True)
        cell_ids = lax.broadcasted_iota(jnp.int32, (1, cells + 128), 1)
        last_v[...] = jnp.sum((cell_c < cell_ids).astype(jnp.int32), axis=0, keepdims=True)
        to_smem = [pltpu.make_async_copy(code_v, code, smem_sem.at[0]),
                   pltpu.make_async_copy(last_v, last, smem_sem.at[1])]
        for copy in to_smem:
            copy.start()
    with jax.named_scope("S03proj"):
        for copy in inputs[2:]:
            copy.wait()
        proj[c] = jnp.dot(features[...], weight[...], preferred_element_type=F32).astype(BF16)
        feat_t[...] = features[...].astype(F32).T.astype(BF16)
        cots_t[r] = cots[r].astype(F32).T.astype(BF16)
        sums[0] = jnp.zeros((side, side), F32)
    with jax.named_scope("S04barrier"):
        pl.semaphore_wait(barrier, len(near))

    pending = []

    def gather_send(block, dev):
        copy = remote(proj.at[block], proj.at[block], ag_send.at[len(pending)],
                      ag_recv.at[block], (r, dev))
        copy.start()
        pending.append(copy)

    def gather_wait(block):
        remote(proj.at[block], proj.at[block], ag_send.at[0], ag_recv.at[block],
               (r, c)).wait_recv()

    cot_copies = []
    for d in range(1, R):
        copy = remote(cots.at[r], cots.at[r], cot_send.at[d], cot_recv.at[r], (x_peers[d - 1], c))
        copy.start()
        cot_copies.append(copy)
    for yy in y_peers:
        gather_send(c, col_of(z, yy, k))
    for zz in z_peers:
        gather_send(c, col_of(zz, y, k))
    gather_send(c, col_of(z, y, 1 - k))

    with jax.named_scope("S07loads"):
        for copy in to_smem:
            copy.wait()
        for load in loads:
            load.wait()

    def add_slot(j, acc):
        acc = acc + tile_buf[code[0, j]].astype(F32)
        sums[j + 1] = acc
        return acc

    def pass_on(zz):
        block = col_of(zz, y, k)
        gather_wait(block)
        for yy in y_peers:
            gather_send(block, col_of(z, yy, k))
        gather_send(block, col_of(z, y, 1 - k))

    parts = 8
    early = ()
    acc = jnp.zeros((side, side), F32)
    with jax.named_scope("S08sums"):
        for part in range(parts):
            acc = lax.fori_loop(part * slots // parts, (part + 1) * slots // parts, add_slot, acc,
                                unroll=8)
            for i, at in enumerate(early):
                if at == part and i < len(z_peers):
                    pass_on(z_peers[i])

    with jax.named_scope("S09cot"):
        for d in range(1, R):
            peer = x_peers[d - 1]
            remote(cots.at[peer], cots.at[peer], cot_send.at[d], cot_recv.at[peer], (peer, c)).wait_recv()
            cots_t[peer] = cots[peer].astype(F32).T.astype(BF16)

    kept = dense.shape[0] == C

    def row_block(b, t, start):
        base = b * block_cells + t * per
        parts = []
        for e in range(per):
            end = sums[last[0, base + e + 1]]
            parts.append((end - start).astype(BF16))
            start = end
        return parts, start

    def back_block(b):
        at = b if kept else 0
        start = sums[last[0, b * block_cells]]
        for t in range(row_tiles):
            parts, start = row_block(b, t, start)
            for e in range(per):
                dense[at, t * side:(t + 1) * side, e * side:(e + 1) * side] = parts[e]
        left = jnp.concatenate([cots_t[s] for s in range(R)], axis=1)
        return jnp.dot(left, dense[at], preferred_element_type=F32)

    def far_first(i):
        if O == 1:
            return z
        late = (2 * z) // O
        up = i + (i - z + O) // O
        down = O - 1 - i
        down = down - (z - down + O) // O
        return late * up + (1 - late) * down

    def z_order(i):
        own = i // (O - 1) if O > 1 else 1
        return own * z + (1 - own) * far_first(lax.rem(i, O - 1)) if O > 1 else z

    def place(i):
        return z_order(lax.rem(i, O)), lax.rem(y + i // O + 1, I)

    def sib_copy(m):
        return remote(sib_out.at[m], sib_in.at[m], sib_send.at[m], sib_recv.at[m],
                      (r, col_of(z, y, 1 - k)))

    def send_sib(i, carry):
        zz, yy = place(i)
        m = zz * I + yy
        sib_out[m] = back_block(2 * m + 1 - k).astype(BF16)
        sib_copy(m).start()
        return carry

    def y_copy(zz, yy):
        return remote(y_out.at[zz * I + yy], y_in.at[y * O + zz], y_send.at[zz * I + yy],
                      y_recv.at[y * O + zz], (r, col_of(z, yy, k)))

    def send_y(i, carry):
        zz, yy = place(i)
        m = zz * I + yy
        mine = back_block(2 * m + k)
        sib_copy(m).wait_recv()
        y_out[m] = (mine + sib_in[m].astype(F32)).astype(BF16)
        y_copy(zz, yy).start()
        return carry

    with jax.named_scope("S10sib"):
        lax.fori_loop(0, O * (I - 1), send_sib, 0)
    with jax.named_scope("S11y"):
        lax.fori_loop(0, O * (I - 1), send_y, 0)
    with jax.named_scope("S12agfwda"):
        for zz in z_peers[len(early):2]:
            pass_on(zz)
    with jax.named_scope("S12sib"):
        lax.fori_loop(O * (I - 1), O * I, send_sib, 0)
    with jax.named_scope("S12agfwdb"):
        for zz in z_peers[2:]:
            pass_on(zz)

    def summed(zz):
        m = zz * I + y
        value = back_block(2 * m + k)
        sib_copy(m).wait_recv()
        value = value + sib_in[m].astype(F32)
        for yy in y_peers:
            slot = yy * O + zz
            remote(y_out.at[0], y_in.at[slot], y_send.at[0], y_recv.at[slot],
                   (r, c)).wait_recv()
            value = value + y_in[slot].astype(F32)
        return value

    z_copies = []
    with jax.named_scope("S13z"):
        for d in range(O - 1):
            zz = z_order(d)
            z_out[d] = summed(zz).astype(BF16)
            copy = remote(z_out.at[d], z_in.at[z], z_send.at[d], z_recv.at[z],
                          (r, col_of(zz, y, k)))
            copy.start()
            z_copies.append(copy)
    with jax.named_scope("S17own"):
        back_t = summed(z)
    with jax.named_scope("S18zwait"):
        for zz in z_peers:
            remote(z_out.at[0], z_in.at[zz], z_send.at[0], z_recv.at[zz], (r, c)).wait_recv()
            back_t = back_t + z_in[zz].astype(F32)
    with jax.named_scope("S19term"):
        back = back_t.T.astype(BF16)
        term = jnp.dot(feat_t[...], back, preferred_element_type=F32)
        term_out[...] = term.reshape(term_out.shape).astype(BF16)

    owners = term_out.shape[0]
    z_low, z_count = ((O - 1) // 2, 2) if O % 2 == 0 else (O // 2, 1)
    group = z_count * I * 2

    def owner_device(o):
        kk = lax.rem(o, 2)
        yy = lax.rem(o // 2, I)
        zz = z_low + lax.rem(o // (2 * I), z_count)
        return o // group, col_of(zz, yy, kk)

    mine_o = ((r * z_count + z - z_low) * I + y) * 2 + k
    is_owner = (z >= z_low) & (z < z_low + z_count) & (mine_o < owners)

    def term_copy(o):
        return remote(term_out.at[o], term_in.at[me], term_send.at[0], term_recv.at[0],
                      owner_device(o))

    def bulk(count, send, recv):
        part = term_in.at[pl.ds(0, count)]
        return remote(part, part, send.at[0], recv.at[0], (r, c))

    def by_role(act):
        pl.when(is_owner)(lambda: act(owners - 1))
        pl.when(jnp.logical_not(is_owner))(lambda: act(owners))

    def tot_copy(t):
        return remote(total.at[mine_o], total.at[mine_o], tot_send.at[0], tot_recv.at[0],
                      (t // C, lax.rem(t, C)))

    with jax.named_scope("S20termsend"):
        @pl.when(is_owner)
        def _():
            def body(d, carry):
                term_copy(lax.rem(mine_o + d, owners)).start()
                return carry
            lax.fori_loop(1, owners, body, 0, unroll=owners - 1 if owners > 1 else 1)
            term_in[me] = term_out[mine_o]

        @pl.when(jnp.logical_not(is_owner))
        def _():
            def body(d, carry):
                term_copy(lax.rem(me + d, owners)).start()
                return carry
            lax.fori_loop(0, owners, body, 0, unroll=owners)

    with jax.named_scope("S21gf"):
        grad_features[...] = lax.dot_general(
            back, weight[...], (((1,), (1,)), ((), ())), preferred_element_type=F32).astype(BF16)

    with jax.named_scope("S22agfwd"):
        for d in range(O):
            zz = lax.rem(z + d, O)
            for yy in y_peers:
                block = col_of(zz, yy, k)
                gather_wait(block)
                gather_send(block, col_of(z, y, 1 - k))
    with jax.named_scope("S23agwait"):
        for d in range(O):
            for e in range(I):
                gather_wait(col_of(lax.rem(z + d, O), lax.rem(y + e, I), 1 - k))

    wide = 4 if C % 4 == 0 else 1

    def forward(s):
        rows_of = pl.ds(pl.multiple_of(s * stretch, stretch), stretch)

        def stretch_block(b):
            if kept:
                return dense[b, rows_of, :]
            blocks = []
            for a in range(per):
                t = s * per + a
                parts, _ = row_block(b, t, sums[last[0, b * block_cells + t * per]])
                blocks.append(jnp.concatenate(parts, axis=1))
            return jnp.concatenate(blocks, axis=0)

        def step(g, out):
            left = jnp.concatenate([stretch_block(g * wide + b) for b in range(wide)], axis=1)
            right = jnp.concatenate([proj[g * wide + b] for b in range(wide)], axis=0)
            return out + jnp.dot(left, right, preferred_element_type=F32)
        return lax.fori_loop(0, C // wide, step, jnp.zeros((stretch, proj.shape[2]), F32))

    log_copies = []
    with jax.named_scope("S24fwdpeer"):
        for d in range(1, R):
            peer = x_peers[d - 1]
            log_out[d - 1] = forward(peer).astype(BF16)
            copy = remote(log_out.at[d - 1], log_in.at[r], log_send.at[d], log_recv.at[r], (peer, c))
            copy.start()
            log_copies.append(copy)

    with jax.named_scope("S25own"):
        @pl.when(is_owner)
        def _():
            bulk(n - 1, term_send, term_recv).wait_recv()
            whole = jnp.sum(term_in[...].astype(F32), axis=0) * (1.0 / math.sqrt(n * stretch))
            total[mine_o] = whole.astype(BF16)

            def body(d, carry):
                tot_copy(lax.rem(me + d, n)).start()
                return carry
            lax.fori_loop(1, n, body, 0, unroll=n - 1 if n <= 32 else 1)

    with jax.named_scope("S26fwdme"):
        mine_log = forward(r)
    with jax.named_scope("S27log"):
        for d in range(1, R):
            peer = x_peers[d - 1]
            remote(log_out.at[0], log_in.at[peer], log_send.at[0], log_recv.at[peer],
                   (peer, c)).wait_recv()
            mine_log = mine_log + log_in[peer].astype(F32)
        logits[...] = mine_log.astype(BF16)
    with jax.named_scope("S28drain"):
        for copy in pending + cot_copies + log_copies + z_copies:
            copy.wait_send()

        def drain_sib(m, carry):
            sib_copy(m).wait_send()
            return carry

        lax.fori_loop(0, O * I, drain_sib, 0)

        def drain_y(i, carry):
            zz, yy = place(i)
            y_copy(zz, yy).wait_send()
            return carry

        lax.fori_loop(0, O * (I - 1), drain_y, 0)
        by_role(lambda count: bulk(count, term_send, term_recv).wait_send())
    with jax.named_scope("S29totwait"):
        by_role(lambda count: bulk(count, tot_send, tot_recv).wait_recv())
    with jax.named_scope("S30end"):
        grad_weight[...] = total[...].astype(F32).reshape(grad_weight.shape)

        @pl.when(is_owner)
        def _():
            bulk(n - 1, tot_send, tot_recv).wait_send()


def hand_over(a, b, c, x, y, z):
    x[...] = a[...]
    y[...] = b[...]
    z[...] = c[...]


def per_device(R, C, features, weight, tiles, slot_tile_row, tile_cols, live_tiles, cotangent):
    slots, side = tiles.shape[2], tiles.shape[3]
    stretch, width = features.shape
    out_width = weight.shape[1]
    half = C // 2
    O = 4 if half % 4 == 0 else half
    I = half // O
    n = R * C
    per = stretch // side
    cells = R * per * C * per
    centre = R * (2 if O % 2 == 0 else 1) * I * 2
    owners = min(centre, width // 16)
    rows = width // owners
    chunks = 8 if slots % 8 == 0 else 1
    dma = pltpu.SemaphoreType.DMA
    vmem = pltpu.VMEM
    blk = (out_width, stretch)
    gathers = (O - 1) + (I - 1) + 1 + (O - 1) * I + O * (I - 1)
    scratch = [
        vmem((stretch, width), BF16),
        vmem((width, out_width), BF16),
        vmem((1, slots), jnp.int32),
        vmem((1, slots), jnp.int32),
        vmem((slots, side, side), BF16),
        vmem((slots + 1, side, side), F32),
        vmem((C if C * R <= 64 else 1, R * stretch, stretch), BF16),
        vmem((C, stretch, out_width), BF16),
        vmem((R, stretch, out_width), BF16),
        vmem((R,) + blk, BF16),
        vmem((width, stretch), BF16),
        vmem((1, slots), jnp.int32),
        vmem((1, cells + 128), jnp.int32),
        pltpu.SMEM((1, slots), jnp.int32),
        pltpu.SMEM((1, cells + 128), jnp.int32),
        vmem((half,) + blk, BF16),
        vmem((half,) + blk, BF16),
        vmem((half,) + blk, BF16),
        vmem((half,) + blk, BF16),
        vmem((max(O - 1, 1),) + blk, BF16),
        vmem((O,) + blk, BF16),
        vmem((max(R - 1, 1), stretch, out_width), BF16),
        vmem((R, stretch, out_width), BF16),
        vmem((owners, rows, out_width), BF16),
        vmem((n, rows, out_width), BF16),
        vmem((owners, rows, out_width), BF16),
        dma((chunks,)), dma((5,)), dma((2,)), dma((R,)), dma((R,)),
        dma((gathers,)), dma((C,)),
        dma((half,)), dma((half,)), dma((half,)), dma((half,)),
        dma((O,)), dma((O,)), dma((R,)), dma((R,)),
        dma((1,)), dma((1,)), dma((1,)), dma((1,)),
    ]
    v = pl.BlockSpec(memory_space=pltpu.VMEM)
    hbm = pl.BlockSpec(memory_space=pltpu.HBM)
    shapes = (
            jax.ShapeDtypeStruct((stretch, out_width), BF16),
            jax.ShapeDtypeStruct((stretch, width), BF16),
            jax.ShapeDtypeStruct((width, out_width), F32),
        )

    def in_hbm(x):
        return pltpu.with_memory_space_constraint(x, pltpu.HBM)

    results = pl.pallas_call(
        functools.partial(kernel, (R, C, O, I)),
        out_shape=tuple(vmem(s.shape, s.dtype) for s in shapes),
        in_specs=[hbm] * 5 + [pl.BlockSpec(memory_space=pltpu.SMEM), hbm],
        out_specs=(v, v, v),
        scratch_shapes=scratch,
        compiler_params=pltpu.CompilerParams(
            collective_id=0, has_side_effects=True, vmem_limit_bytes=52 * 1024 * 1024),
    )(in_hbm(features), in_hbm(weight), in_hbm(tiles.reshape(slots, side, side)),
      in_hbm(slot_tile_row.reshape(1, slots)), in_hbm(tile_cols.reshape(1, slots)), live_tiles,
      in_hbm(cotangent))
    results = [pltpu.with_memory_space_constraint(x, pltpu.VMEM) for x in results]
    return pl.pallas_call(hand_over, out_shape=shapes, in_specs=[v, v, v],
                          out_specs=(v, v, v))(*results)


def solution(mesh):
    R, C = mesh.shape["row"], mesh.shape["col"]
    placed = (
        P(("row", "col"), None),
        P(),
        P("row", "col", None, None, None),
        P("row", "col", None),
        P("row", "col", None),
        P("row", "col"),
        P(("row", "col"), None),
    )
    return jax.shard_map(
        functools.partial(per_device, R, C),
        mesh=mesh,
        in_specs=placed,
        out_specs=(P(("row", "col"), None), P(("row", "col"), None), P()),
        check_vma=False,
    )
```

time: 43.2 us -> 34.1 us (0.79)
  Pallas kernels: 41.8 us -> 32.6 us
    pallas_call x1, Pallas kernels: 40 us -> 31.9 us  [per_device(): pl.pallas_call(functools.partial(kernel, (R, C, O, I)), out_shape=tuple((...]
    pallas_call x1, Pallas kernels: 1.73 us -> 0.74 us  [per_device(): pl.pallas_call(hand_over, out_shape=shapes, in_specs=[v, v, v], out_specs...]
where the time goes in v1:
time: 34.1 us; the launch traced here: 33.9 us
  Pallas kernels  32.6 us (96%)
  between operations  1.29 us (4%)
    pallas_call x1, Pallas kernels, per_device(): pl.pallas_call(functools.partial(kernel, (R, C, O, I)), out_shape=tuple((...  31.9 us
    pallas_call x1, Pallas kernels, per_device(): pl.pallas_call(hand_over, out_shape=shapes, in_specs=[v, v, v], out_specs...  0.74 us

profile of v1, /device:TPU:0, one launch (start us, length us, event | category | flops | bytes accessed | tf_op | source)
XLA Modules:
  0.0 33.9 jit_solution(5475672975146490669)
XLA Ops:
  1.3 31.9 %shard_map.94 = (bf16[256,128]{1,0:T(8,128)(2,1)S(1)}, bf16[256,256]{1,0:T(8,128)(2,1)S(1)}, f32[256,128]{1,0:T(8,128)S(1)}) custom-call(bf16[256,256]{1,0:T(8,128)(2,1)} %features_h.1, bf16[256,128]{1,0:T(8,128)(2,1)} %weight_h.1, bf16[320,128,128]{2,1,0:T(8,128)(2,1)} %bitcast.3, s32[1,320]{1,0:T(1,128)} %bitcast.4, s32[1,320]{1,0:T(1,128)} %bitcast.5, ...), custom_call_target="tpu_custom_call" | custom-call | tf_op jit(solution)/shard_map/pallas_call | solution.py:482
  33.1 0.7 %shard_map.95 = (bf16[256,128]{1,0:T(8,128)(2,1)}, bf16[256,256]{1,0:T(8,128)(2,1)}, f32[256,128]{1,0:T(8,128)}) custom-call(bf16[256,128]{1,0:T(8,128)(2,1)S(1)} %get-tuple-element.6.a, bf16[256,256]{1,0:T(8,128)(2,1)S(1)} %get-tuple-element.7.b, f32[256,128]{1,0:T(8,128)S(1)} %get-tuple-element.8.c), custom_call_target="tpu_custom_call" | custom-call | tf_op jit(solution)/shard_map/pallas_call | solution.py:494

commit v2 on v1

--- a/solution.py
+++ b/solution.py
@@ -17,10 +17,10 @@
            logits, grad_features, grad_weight,
            features, weight, slot_rows, slot_cols,
            tile_buf, sums, dense, proj, cots, cots_t, feat_t, code_v, last_v, code, last,
-           sib_out, sib_in, y_out, y_in, z_out, z_in, log_out, log_in,
+           sib_out, sib_in, y_out, y_in, p_out, p_in, z_out, z_in, log_out, log_in, far_feat,
            term_out, term_in, total,
            tile_sem, in_sem, smem_sem, cot_send, cot_recv, ag_send, ag_recv,
-           sib_send, sib_recv, y_send, y_recv, z_send, z_recv,
+           sib_send, sib_recv, y_send, y_recv, p_send, p_recv, z_send, z_recv, far_send, far_recv,
            log_send, log_recv, term_send, term_recv, tot_send, tot_recv):
     R, C, O, I = dims
     n = R * C
@@ -37,6 +37,9 @@
     q = c // 2
     y = lax.rem(q, I)
     z = q // I
+    H = O // 2
+    zl = lax.rem(z, 2)
+    zh = z // 2
 
     def col_of(zz, yy, kk):
         return (zz * I + yy) * 2 + kk
@@ -62,11 +65,14 @@
         for i in range(chunks)
     ]
     for load in loads[:0]:
-        load.start()
+        load.start(priority=0)
 
     x_peers = [lax.rem(r + d, R) for d in range(1, R)]
     y_peers = [lax.rem(y + d, I) for d in range(1, I)]
-    z_peers = [lax.rem(z + d, O) for d in range(1, O)]
+    partner = 2 * zh + 1 - zl
+    odd_peers = [2 * lax.rem(zh + d, H) + 1 - zl for d in range(H)]
+    even_peers = [2 * lax.rem(zh + d, H) + zl for d in range(1, H)]
+    z_peers = odd_peers + even_peers
     near = ([(peer, c) for peer in x_peers] + [(r, col_of(z, yy, k)) for yy in y_peers]
             + [(r, col_of(zz, y, k)) for zz in z_peers] + [(r, col_of(z, y, 1 - k))])
     barrier = pltpu.get_barrier_semaphore()
@@ -79,7 +85,7 @@
             copy.wait()
     with jax.named_scope("S01rest"):
         for load in loads[0:]:
-            load.start()
+            load.start(priority=0)
     with jax.named_scope("S02sort"):
         lane = lax.broadcasted_iota(jnp.int32, (1, slots), 1)
         col = slot_cols[...]
@@ -102,18 +108,19 @@
         for copy in inputs[2:]:
             copy.wait()
         proj[c] = jnp.dot(features[...], weight[...], preferred_element_type=F32).astype(BF16)
-        feat_t[...] = features[...].astype(F32).T.astype(BF16)
+        feat_t[0] = features[...].astype(F32).T.astype(BF16)
         cots_t[r] = cots[r].astype(F32).T.astype(BF16)
         sums[0] = jnp.zeros((side, side), F32)
     with jax.named_scope("S04barrier"):
         pl.semaphore_wait(barrier, len(near))
 
     pending = []
+    pending_far = []
 
     def gather_send(block, dev):
         copy = remote(proj.at[block], proj.at[block], ag_send.at[len(pending)],
                       ag_recv.at[block], (r, dev))
-        copy.start()
+        copy.start(priority=0)
         pending.append(copy)
 
     def gather_wait(block):
@@ -123,12 +130,16 @@
     cot_copies = []
     for d in range(1, R):
         copy = remote(cots.at[r], cots.at[r], cot_send.at[d], cot_recv.at[r], (x_peers[d - 1], c))
-        copy.start()
+        copy.start(priority=0)
         cot_copies.append(copy)
     for yy in y_peers:
         gather_send(c, col_of(z, yy, k))
-    for zz in z_peers:
+    for zz in odd_peers:
         gather_send(c, col_of(zz, y, k))
+    for i, zz in enumerate(even_peers):
+        copy = remote(features, far_feat.at[zh], far_send.at[i], far_recv.at[zh], (r, col_of(zz, y, k)))
+        copy.start(priority=0)
+        pending_far.append(copy)
     gather_send(c, col_of(z, y, 1 - k))
 
     with jax.named_scope("S07loads"):
@@ -142,15 +153,22 @@
         sums[j + 1] = acc
         return acc
 
-    def pass_on(zz):
+    def pass_on(i):
+        zz = z_peers[i]
         block = col_of(zz, y, k)
-        gather_wait(block)
+        if i < H:
+            gather_wait(block)
+        else:
+            hh = lax.rem(zh + i - H + 1, H)
+            remote(features, far_feat.at[hh], far_send.at[0], far_recv.at[hh], (r, c)).wait_recv()
+            proj[block] = jnp.dot(far_feat[hh], weight[...], preferred_element_type=F32).astype(BF16)
+            feat_t[i - H + 1] = far_feat[hh].astype(F32).T.astype(BF16)
         for yy in y_peers:
             gather_send(block, col_of(z, yy, k))
         gather_send(block, col_of(z, y, 1 - k))
 
     parts = 8
-    early = ()
+    early = (7,)
     acc = jnp.zeros((side, side), F32)
     with jax.named_scope("S08sums"):
         for part in range(parts):
@@ -158,7 +176,7 @@
                                 unroll=8)
             for i, at in enumerate(early):
                 if at == part and i < len(z_peers):
-                    pass_on(z_peers[i])
+                    pass_on(i)
 
     with jax.named_scope("S09cot"):
         for d in range(1, R):
@@ -187,18 +205,10 @@
         left = jnp.concatenate([cots_t[s] for s in range(R)], axis=1)
         return jnp.dot(left, dense[at], preferred_element_type=F32)
 
-    def far_first(i):
-        if O == 1:
-            return z
-        late = (2 * z) // O
-        up = i + (i - z + O) // O
-        down = O - 1 - i
-        down = down - (z - down + O) // O
-        return late * up + (1 - late) * down
-
     def z_order(i):
-        own = i // (O - 1) if O > 1 else 1
-        return own * z + (1 - own) * far_first(lax.rem(i, O - 1)) if O > 1 else z
+        late = i // H
+        same = late * zl + (1 - late) * (1 - zl)
+        return 2 * lax.rem(zh + 1 + lax.rem(i, H), H) + same
 
     def place(i):
         return z_order(lax.rem(i, O)), lax.rem(y + i // O + 1, I)
@@ -232,13 +242,13 @@
     with jax.named_scope("S11y"):
         lax.fori_loop(0, O * (I - 1), send_y, 0)
     with jax.named_scope("S12agfwda"):
-        for zz in z_peers[len(early):2]:
-            pass_on(zz)
+        for i in range(len(early), 2):
+            pass_on(i)
     with jax.named_scope("S12sib"):
         lax.fori_loop(O * (I - 1), O * I, send_sib, 0)
     with jax.named_scope("S12agfwdb"):
-        for zz in z_peers[2:]:
-            pass_on(zz)
+        for i in range(max(2, len(early)), O - 1):
+            pass_on(i)
 
     def summed(zz):
         m = zz * I + y
@@ -253,27 +263,39 @@
         return value
 
     z_copies = []
-    with jax.named_scope("S13z"):
-        for d in range(O - 1):
-            zz = z_order(d)
-            z_out[d] = summed(zz).astype(BF16)
-            copy = remote(z_out.at[d], z_in.at[z], z_send.at[d], z_recv.at[z],
-                          (r, col_of(zz, y, k)))
+    with jax.named_scope("S13p"):
+        for i in range(H):
+            hh = lax.rem(zh + 1 + i, H)
+            p_out[i] = summed(z_order(i)).astype(BF16)
+            copy = remote(p_out.at[i], p_in.at[hh], p_send.at[i], p_recv.at[hh],
+                          (r, col_of(partner, y, k)))
             copy.start()
             z_copies.append(copy)
-    with jax.named_scope("S17own"):
-        back_t = summed(z)
-    with jax.named_scope("S18zwait"):
-        for zz in z_peers:
-            remote(z_out.at[0], z_in.at[zz], z_send.at[0], z_recv.at[zz], (r, c)).wait_recv()
-            back_t = back_t + z_in[zz].astype(F32)
+    lefts, rights = [feat_t[0]], []
+    for i in range(H):
+        with jax.named_scope("S14own"):
+            hh = lax.rem(zh + 1 + i, H)
+            value = summed(z_order(H + i))
+        with jax.named_scope("S15pwait"):
+            remote(p_out.at[0], p_in.at[hh], p_send.at[0], p_recv.at[hh], (r, c)).wait_recv()
+            value = value + p_in[hh].astype(F32)
+            if i < H - 1:
+                z_out[i] = value.astype(BF16)
+                copy = remote(z_out.at[i], z_in.at[zh], z_send.at[i], z_recv.at[zh],
+                              (r, col_of(2 * hh + zl, y, k)))
+                copy.start()
+                z_copies.append(copy)
+                lefts.append(feat_t[i + 1])
+                rights.append(value.T.astype(BF16))
     with jax.named_scope("S19term"):
-        back = back_t.T.astype(BF16)
-        term = jnp.dot(feat_t[...], back, preferred_element_type=F32)
+        back_t = value
+        rights = [value.T.astype(BF16)] + rights
+        term = jnp.dot(jnp.concatenate(lefts, axis=1), jnp.concatenate(rights, axis=0),
+                       preferred_element_type=F32)
         term_out[...] = term.reshape(term_out.shape).astype(BF16)
 
     owners = term_out.shape[0]
-    z_low, z_count = ((O - 1) // 2, 2) if O % 2 == 0 else (O // 2, 1)
+    z_low, z_count = H - 1, 2
     group = z_count * I * 2
 
     def owner_device(o):
@@ -316,10 +338,6 @@
                 term_copy(lax.rem(me + d, owners)).start()
                 return carry
             lax.fori_loop(0, owners, body, 0, unroll=owners)
-
-    with jax.named_scope("S21gf"):
-        grad_features[...] = lax.dot_general(
-            back, weight[...], (((1,), (1,)), ((), ())), preferred_element_type=F32).astype(BF16)
 
     with jax.named_scope("S22agfwd"):
         for d in range(O):
@@ -375,6 +393,15 @@
                 return carry
             lax.fori_loop(1, n, body, 0, unroll=n - 1 if n <= 32 else 1)
 
+    with jax.named_scope("S26gf"):
+        for i in range(H - 1):
+            hh = lax.rem(zh + 1 + i, H)
+            remote(z_out.at[0], z_in.at[hh], z_send.at[0], z_recv.at[hh], (r, c)).wait_recv()
+            back_t = back_t + z_in[hh].astype(F32)
+        grad_features[...] = lax.dot_general(
+            back_t.T.astype(BF16), weight[...], (((1,), (1,)), ((), ())),
+            preferred_element_type=F32).astype(BF16)
+
     with jax.named_scope("S26fwdme"):
         mine_log = forward(r)
     with jax.named_scope("S27log"):
@@ -385,7 +412,7 @@
             mine_log = mine_log + log_in[peer].astype(F32)
         logits[...] = mine_log.astype(BF16)
     with jax.named_scope("S28drain"):
-        for copy in pending + cot_copies + log_copies + z_copies:
+        for copy in pending + pending_far + cot_copies + log_copies + z_copies:
             copy.wait_send()
 
         def drain_sib(m, carry):
@@ -422,12 +449,13 @@
     stretch, width = features.shape
     out_width = weight.shape[1]
     half = C // 2
-    O = 4 if half % 4 == 0 else half
+    O = 4 if half % 4 == 0 else 2
+    H = O // 2
     I = half // O
     n = R * C
     per = stretch // side
     cells = R * per * C * per
-    centre = R * (2 if O % 2 == 0 else 1) * I * 2
+    centre = R * 2 * I * 2
     owners = min(centre, width // 16)
     rows = width // owners
     chunks = 8 if slots % 8 == 0 else 1
@@ -446,7 +474,7 @@
         vmem((C, stretch, out_width), BF16),
         vmem((R, stretch, out_width), BF16),
         vmem((R,) + blk, BF16),
-        vmem((width, stretch), BF16),
+        vmem((H, width, stretch), BF16),
         vmem((1, slots), jnp.int32),
         vmem((1, cells + 128), jnp.int32),
         pltpu.SMEM((1, slots), jnp.int32),
@@ -455,17 +483,20 @@
         vmem((half,) + blk, BF16),
         vmem((half,) + blk, BF16),
         vmem((half,) + blk, BF16),
-        vmem((max(O - 1, 1),) + blk, BF16),
-        vmem((O,) + blk, BF16),
+        vmem((H,) + blk, BF16),
+        vmem((H,) + blk, BF16),
+        vmem((H,) + blk, BF16),
+        vmem((H,) + blk, BF16),
         vmem((max(R - 1, 1), stretch, out_width), BF16),
         vmem((R, stretch, out_width), BF16),
+        vmem((H, stretch, width), BF16),
         vmem((owners, rows, out_width), BF16),
         vmem((n, rows, out_width), BF16),
         vmem((owners, rows, out_width), BF16),
         dma((chunks,)), dma((5,)), dma((2,)), dma((R,)), dma((R,)),
         dma((gathers,)), dma((C,)),
         dma((half,)), dma((half,)), dma((half,)), dma((half,)),
-        dma((O,)), dma((O,)), dma((R,)), dma((R,)),
+        dma((H,)), dma((H,)), dma((H,)), dma((H,)), dma((H,)), dma((H,)), dma((R,)), dma((R,)),
         dma((1,)), dma((1,)), dma((1,)), dma((1,)),
     ]
     v = pl.BlockSpec(memory_space=pltpu.VMEM)

time: 34.1 us -> 32.7 us (0.959)
  Pallas kernels: 32.6 us -> 31.2 us
    pallas_call x1, Pallas kernels: 31.9 us -> 30.5 us  [per_device(): pl.pallas_call(functools.partial(kernel, (R, C, O, I)), out_shape=tuple((...]
where the time goes in v2:
time: 32.7 us; the launch traced here: 32.5 us
  Pallas kernels  31.2 us (95%)
  between operations  1.29 us (4%)
    pallas_call x1, Pallas kernels, per_device(): pl.pallas_call(functools.partial(kernel, (R, C, O, I)), out_shape=tuple((...  30.5 us
    pallas_call x1, Pallas kernels, per_device(): pl.pallas_call(hand_over, out_shape=shapes, in_specs=[v, v, v], out_specs...  0.74 us

profile of v2, /device:TPU:0, one launch (start us, length us, event | category | flops | bytes accessed | tf_op | source)
XLA Modules:
  0.0 32.5 jit_solution(15193607740680262842)
XLA Ops:
  1.3 30.5 %shard_map.94 = (bf16[256,128]{1,0:T(8,128)(2,1)S(1)}, bf16[256,256]{1,0:T(8,128)(2,1)S(1)}, f32[256,128]{1,0:T(8,128)S(1)}) custom-call(bf16[256,256]{1,0:T(8,128)(2,1)} %features_h.1, bf16[256,128]{1,0:T(8,128)(2,1)} %weight_h.1, bf16[320,128,128]{2,1,0:T(8,128)(2,1)} %bitcast.3, s32[1,320]{1,0:T(1,128)} %bitcast.4, s32[1,320]{1,0:T(1,128)} %bitcast.5, ...), custom_call_target="tpu_custom_call" | custom-call | tf_op jit(solution)/shard_map/pallas_call | solution.py:513
  31.8 0.7 %shard_map.95 = (bf16[256,128]{1,0:T(8,128)(2,1)}, bf16[256,256]{1,0:T(8,128)(2,1)}, f32[256,128]{1,0:T(8,128)}) custom-call(bf16[256,128]{1,0:T(8,128)(2,1)S(1)} %get-tuple-element.6.a, bf16[256,256]{1,0:T(8,128)(2,1)S(1)} %get-tuple-element.7.b, f32[256,128]{1,0:T(8,128)S(1)} %get-tuple-element.8.c), custom_call_target="tpu_custom_call" | custom-call | tf_op jit(solution)/shard_map/pallas_call | solution.py:525

commit v3 on v2

--- a/solution.py
+++ b/solution.py
@@ -64,8 +64,8 @@
                               tile_buf.at[pl.ds(i * chunk, chunk)], tile_sem.at[i])
         for i in range(chunks)
     ]
-    for load in loads[:0]:
-        load.start(priority=0)
+    for load in loads[:8]:
+        load.start(priority=1)
 
     x_peers = [lax.rem(r + d, R) for d in range(1, R)]
     y_peers = [lax.rem(y + d, I) for d in range(1, I)]
@@ -73,8 +73,9 @@
     odd_peers = [2 * lax.rem(zh + d, H) + 1 - zl for d in range(H)]
     even_peers = [2 * lax.rem(zh + d, H) + zl for d in range(1, H)]
     z_peers = odd_peers + even_peers
+    z_near = z_peers
     near = ([(peer, c) for peer in x_peers] + [(r, col_of(z, yy, k)) for yy in y_peers]
-            + [(r, col_of(zz, y, k)) for zz in z_peers] + [(r, col_of(z, y, 1 - k))])
+            + [(r, col_of(zz, y, k)) for zz in z_near] + [(r, col_of(z, y, 1 - k))])
     barrier = pltpu.get_barrier_semaphore()
     with jax.named_scope("S00greet"):
         for dev in near:
@@ -84,8 +85,8 @@
         for copy in inputs[:2]:
             copy.wait()
     with jax.named_scope("S01rest"):
-        for load in loads[0:]:
-            load.start(priority=0)
+        for load in loads[8:8]:
+            load.start(priority=1)
     with jax.named_scope("S02sort"):
         lane = lax.broadcasted_iota(jnp.int32, (1, slots), 1)
         col = slot_cols[...]
@@ -134,7 +135,7 @@
         cot_copies.append(copy)
     for yy in y_peers:
         gather_send(c, col_of(z, yy, k))
-    for zz in odd_peers:
+    for zz in odd_peers[:H]:
         gather_send(c, col_of(zz, y, k))
     for i, zz in enumerate(even_peers):
         copy = remote(features, far_feat.at[zh], far_send.at[i], far_recv.at[zh], (r, col_of(zz, y, k)))
@@ -142,6 +143,8 @@
         pending_far.append(copy)
     gather_send(c, col_of(z, y, 1 - k))
 
+    for load in loads[8:]:
+        load.start(priority=1)
     with jax.named_scope("S07loads"):
         for copy in to_smem:
             copy.wait()
@@ -165,10 +168,13 @@
             feat_t[i - H + 1] = far_feat[hh].astype(F32).T.astype(BF16)
         for yy in y_peers:
             gather_send(block, col_of(z, yy, k))
+        if False and i == 0:
+            for peer in even_peers:
+                gather_send(block, col_of(peer, y, k))
         gather_send(block, col_of(z, y, 1 - k))
 
     parts = 8
-    early = (7,)
+    early = ()
     acc = jnp.zeros((side, side), F32)
     with jax.named_scope("S08sums"):
         for part in range(parts):
@@ -247,7 +253,7 @@
     with jax.named_scope("S12sib"):
         lax.fori_loop(O * (I - 1), O * I, send_sib, 0)
     with jax.named_scope("S12agfwdb"):
-        for i in range(max(2, len(early)), O - 1):
+        for i in range(max(2, len(early)), 2):
             pass_on(i)
 
     def summed(zz):
@@ -271,7 +277,11 @@
                           (r, col_of(partner, y, k)))
             copy.start()
             z_copies.append(copy)
-    lefts, rights = [feat_t[0]], []
+    with jax.named_scope("S13late"):
+        for i in range(2, O - 1):
+            pass_on(i)
+    term = jnp.zeros((feat_t.shape[1], proj.shape[2]), F32)
+    z_late = []
     for i in range(H):
         with jax.named_scope("S14own"):
             hh = lax.rem(zh + 1 + i, H)
@@ -283,15 +293,15 @@
                 z_out[i] = value.astype(BF16)
                 copy = remote(z_out.at[i], z_in.at[zh], z_send.at[i], z_recv.at[zh],
                               (r, col_of(2 * hh + zl, y, k)))
-                copy.start()
+                if False:
+                    z_late.append(copy)
+                else:
+                    copy.start()
                 z_copies.append(copy)
-                lefts.append(feat_t[i + 1])
-                rights.append(value.T.astype(BF16))
+                term = term + jnp.dot(feat_t[i + 1], value.T.astype(BF16), preferred_element_type=F32)
     with jax.named_scope("S19term"):
         back_t = value
-        rights = [value.T.astype(BF16)] + rights
-        term = jnp.dot(jnp.concatenate(lefts, axis=1), jnp.concatenate(rights, axis=0),
-                       preferred_element_type=F32)
+        term = term + jnp.dot(feat_t[0], value.T.astype(BF16), preferred_element_type=F32)
         term_out[...] = term.reshape(term_out.shape).astype(BF16)
 
     owners = term_out.shape[0]
@@ -339,6 +349,8 @@
                 return carry
             lax.fori_loop(0, owners, body, 0, unroll=owners)
 
+    for copy in z_late:
+        copy.start()
     with jax.named_scope("S22agfwd"):
         for d in range(O):
             zz = lax.rem(z + d, O)
@@ -393,15 +405,6 @@
                 return carry
             lax.fori_loop(1, n, body, 0, unroll=n - 1 if n <= 32 else 1)
 
-    with jax.named_scope("S26gf"):
-        for i in range(H - 1):
-            hh = lax.rem(zh + 1 + i, H)
-            remote(z_out.at[0], z_in.at[hh], z_send.at[0], z_recv.at[hh], (r, c)).wait_recv()
-            back_t = back_t + z_in[hh].astype(F32)
-        grad_features[...] = lax.dot_general(
-            back_t.T.astype(BF16), weight[...], (((1,), (1,)), ((), ())),
-            preferred_element_type=F32).astype(BF16)
-
     with jax.named_scope("S26fwdme"):
         mine_log = forward(r)
     with jax.named_scope("S27log"):
@@ -411,6 +414,15 @@
                    (peer, c)).wait_recv()
             mine_log = mine_log + log_in[peer].astype(F32)
         logits[...] = mine_log.astype(BF16)
+    with jax.named_scope("S26gf"):
+        for i in range(H - 1):
+            hh = lax.rem(zh + 1 + i, H)
+            remote(z_out.at[0], z_in.at[hh], z_send.at[0], z_recv.at[hh], (r, c)).wait_recv()
+            back_t = back_t + z_in[hh].astype(F32)
+        grad_features[...] = lax.dot_general(
+            back_t.T.astype(BF16), weight[...], (((1,), (1,)), ((), ())),
+            preferred_element_type=F32).astype(BF16)
+
     with jax.named_scope("S28drain"):
         for copy in pending + pending_far + cot_copies + log_copies + z_copies:
             copy.wait_send()

time: 32.7 us -> 32.1 us (0.982)
  Pallas kernels: 31.2 us -> 30.7 us
    pallas_call x1, Pallas kernels: 30.5 us -> 30 us  [per_device(): pl.pallas_call(functools.partial(kernel, (R, C, O, I)), out_shape=tuple((...]
where the time goes in v3:
time: 32.1 us; the launch traced here: 32 us
  Pallas kernels  30.7 us (96%)
  between operations  1.29 us (4%)
    pallas_call x1, Pallas kernels, per_device(): pl.pallas_call(functools.partial(kernel, (R, C, O, I)), out_shape=tuple((...  30 us
    pallas_call x1, Pallas kernels, per_device(): pl.pallas_call(hand_over, out_shape=shapes, in_specs=[v, v, v], out_specs...  0.74 us

profile of v3, /device:TPU:0, one launch (start us, length us, event | category | flops | bytes accessed | tf_op | source)
XLA Modules:
  0.0 32.0 jit_solution(8636254631652218399)
XLA Ops:
  1.3 30.0 %shard_map.94 = (bf16[256,128]{1,0:T(8,128)(2,1)S(1)}, bf16[256,256]{1,0:T(8,128)(2,1)S(1)}, f32[256,128]{1,0:T(8,128)S(1)}) custom-call(bf16[256,256]{1,0:T(8,128)(2,1)} %features_h.1, bf16[256,128]{1,0:T(8,128)(2,1)} %weight_h.1, bf16[320,128,128]{2,1,0:T(8,128)(2,1)} %bitcast.3, s32[1,320]{1,0:T(1,128)} %bitcast.4, s32[1,320]{1,0:T(1,128)} %bitcast.5, ...), custom_call_target="tpu_custom_call" | custom-call | tf_op jit(solution)/shard_map/pallas_call | solution.py:525
  31.2 0.7 %shard_map.95 = (bf16[256,128]{1,0:T(8,128)(2,1)}, bf16[256,256]{1,0:T(8,128)(2,1)}, f32[256,128]{1,0:T(8,128)}) custom-call(bf16[256,128]{1,0:T(8,128)(2,1)S(1)} %get-tuple-element.6.a, bf16[256,256]{1,0:T(8,128)(2,1)S(1)} %get-tuple-element.7.b, f32[256,128]{1,0:T(8,128)S(1)} %get-tuple-element.8.c), custom_call_target="tpu_custom_call" | custom-call | tf_op jit(solution)/shard_map/pallas_call | solution.py:537
